TPU v7x, 512 devices: a whole 4x4x16 slice. The times are simulated.
512 devices in a mesh: seq: 64 (over z, x), head: 8 (over y, core).
Axes of the slice: x: 4, y: 4, z: 16, core: 2. Of those that a mesh axis runs over, the one named last changes fastest.
Arguments:
- tokens: bfloat16 [65536, 1024], P('seq'), may hold values from -60 to 60
- qkv_weight: bfloat16 [1024, 8, 384], P(None, 'head'), may hold values from -0.1875 to 0.1875
- out_weight: bfloat16 [8, 128, 1024], P('head'), may hold values from -0.1875 to 0.1875
- members: int32 [8, 256, 768], P('head', None, 'seq'), may hold values from 0 to 65535, as said below
- counts: int32 [8, 64, 256], P('head', 'seq'), may hold values from 1 to 12, as said below
Outputs:
- mixed: bfloat16 [65536, 1024], P(('seq', 'head'))
- centroids: float32 [8, 256, 128], P('head', 'seq')
Inputs may be any that keep to these rules, and one draw needn't show every extreme that they name: `members`: the entries of slots j of any cluster lie in slab j // 12, i.e. in positions 1024 * (j // 12) up to 1024 * (j // 12 + 1) - 1. For each head and slab, the valid entries (j % 12 < counts) over all clusters name every token of that slab exactly once; the other entries are padding with some position of the same slab. For each head and slab the counts over the 256 clusters sum to 1024. For each head, one cluster has 12 members from every slab. Split the 256 clusters into 64 aligned groups of equal size; for each head and slab the counts of one group sum to at most 32, and exactly 32 for the group that holds the full cluster.
All inputs are finite; a program needn't handle non-finite values.
Results may differ from a plain program's by a relative error of at most 0.02.
The roundings to bfloat16 on the way count: a program that leaves them out, or rounds other values in their place, can miss the bound.
Values may be sent and summed in bfloat16 or wider, within the bound.
A program may use at most 128 MiB of HBM per device.

v0:
```python
import jax
import jax.numpy as jnp
from jax import lax
from jax.sharding import PartitionSpec as P

eps_norm = 1e-06


def unit_rows(keys_in):
    widened = keys_in.astype(jnp.float32)
    return widened * lax.rsqrt(jnp.sum(widened * widened, axis=-1, keepdims=True) + eps_norm)


def normalize_rows(sums):
    return sums * lax.rsqrt(jnp.mean(sums * sums, axis=-1, keepdims=True) + eps_norm)


def attend_core(got_rows, got_positions, head_dim, scale):
    seq_count = got_positions.shape[1]
    slab_slots = got_positions.shape[3]
    same_slot = jnp.eye(seq_count * slab_slots, dtype=bool).reshape(
        seq_count, slab_slots, seq_count, slab_slots
    )
    queries = got_rows[..., :head_dim]
    keys_in = got_rows[..., head_dim : 2 * head_dim]
    values_in = got_rows[..., 2 * head_dim :]
    scores = (
        jnp.einsum("hscie,htcje->hcsitj", queries, keys_in, preferred_element_type=jnp.float32)
        * scale
    )
    ordered = jnp.transpose(got_positions, (0, 2, 1, 3))
    query_pos = ordered[:, :, :, :, None, None]
    key_pos = ordered[:, :, None, None, :, :]
    allowed = (key_pos >= 0) & (key_pos <= query_pos) | same_slot[None, None]
    masked = jnp.where(allowed, scores, -1e30)
    highest = jnp.max(masked, axis=(4, 5), keepdims=True)
    expo = jnp.exp(masked - highest)
    probs = (expo / jnp.sum(expo, axis=(4, 5), keepdims=True)).astype(jnp.bfloat16)
    return jnp.einsum(
        "hcsitj,htcje->hscie", probs, values_in, preferred_element_type=jnp.float32
    ).astype(jnp.bfloat16)


def on_device(tokens, qkv_weight, out_weight, members, counts):
    slab_len = tokens.shape[0]
    heads_here = qkv_weight.shape[1]
    head_dim = out_weight.shape[1]
    clusters = members.shape[1]
    slab_slots = members.shape[2]
    seq_count = lax.axis_size("seq")
    owned = clusters // seq_count
    my_slab = lax.axis_index("seq")
    scale = head_dim ** (-0.5)
    projected = jnp.einsum(
        "td,dhe->hte", tokens, qkv_weight, preferred_element_type=jnp.float32
    ).astype(jnp.bfloat16)
    local_ids = members - my_slab * slab_len
    valid = jnp.arange(slab_slots, dtype=jnp.int32)[None, None, :] < counts[:, 0, :, None]
    positions = jnp.where(valid, members, -1)
    member_rows = jax.vmap(lambda table, index: table[index])(projected, local_ids)
    slab_sums = jnp.sum(
        jnp.where(valid[..., None], unit_rows(member_rows[..., head_dim : 2 * head_dim]), 0.0),
        axis=2,
    )
    all_sums = lax.psum(slab_sums, "seq")
    mine = lax.dynamic_slice_in_dim(all_sums, my_slab * owned, owned, 1)
    head_index = jnp.arange(heads_here, dtype=jnp.int32)[:, None, None]
    send_rows = member_rows.reshape(heads_here, seq_count, owned, slab_slots, 3 * head_dim)
    send_positions = positions.reshape(heads_here, seq_count, owned, slab_slots)
    got_rows = lax.all_to_all(send_rows, "seq", split_axis=1, concat_axis=1, tiled=True)
    got_positions = lax.all_to_all(send_positions, "seq", split_axis=1, concat_axis=1, tiled=True)
    attended = attend_core(got_rows, got_positions, head_dim, scale)
    answered = lax.all_to_all(attended, "seq", split_axis=1, concat_axis=1, tiled=True)
    result = answered
    answered = result
    answered = answered.reshape(heads_here, clusters, slab_slots, head_dim)
    target = jnp.where(valid, local_ids, slab_len)
    head_out = (
        jnp.zeros((slab_len, heads_here, head_dim), jnp.bfloat16)
        .at[target, head_index]
        .set(answered, mode="drop")
    )
    centroids = normalize_rows(mine)
    all_heads = lax.all_to_all(head_out, "head", split_axis=0, concat_axis=1, tiled=True)
    mixed = jnp.einsum(
        "the,heo->to",
        all_heads,
        lax.all_gather(out_weight, "head", axis=0, tiled=True),
        preferred_element_type=jnp.float32,
    )
    return (mixed.astype(jnp.bfloat16), centroids)


def solution(mesh):
    return jax.shard_map(
        on_device,
        mesh=mesh,
        in_specs=(
            P("seq", None),
            P(None, "head", None),
            P("head", None, None),
            P("head", None, "seq"),
            P("head", "seq", None),
        ),
        out_specs=(P(("seq", "head"), None), P("head", "seq", None)),
        check_vma=False,
    )
```

profile of v0, /device:TPU:1, one launch (start us, length us, event | category | flops | bytes accessed | tf_op | source)
XLA Modules:
  0.0 421.6 jit_solution(6526205904434901323)
XLA Ops:
  8.0 0.9 compare_select_fusion.2
  8.9 0.8 copy.53
  9.7 19.1 %all-to-all-start.1 = ((s32[1,64,4,12]{3,2,0,1:T(4,128)}), s32[1,64,4,12]{3,2,0,1:T(4,128)S(1)}, u32[]{:S(2)}, u32[]{:S(2)}) async-start(s32[1,64,4,12]{3,2,0,1:T(4,128)} %bitcast.10), calls=%async_computation.1 | async-start | bytes 262144 | tf_op jit(solution)/shard_map/all_to_all | solution.py:71
  28.8 3.0 fusion.5
  32.2 1.5 copy.50
  33.7 29.1 %gather_fusion = bf16[3072,384]{1,0:T(8,128)(2,1)} fusion(bf16[1,1024,384]{2,1,0:T(8,128)(2,1)S(1)} %copy.50, s32[3072]{0:T(1024)S(1)} %reshape.198), kind=kCustom, calls=%fused_computation | custom fusion | bytes 4743168 | tf_op jit(solution)/shard_map/vmap()/gather | solution.py:60
  62.8 5.0 %reshape.180 = bf16[1,64,4,12,384]{4,3,2,1,0:T(8,128)(2,1)} reshape(bf16[3072,384]{1,0:T(8,128)(2,1)} %gather_fusion) | data formatting | bytes 4718592 | tf_op jit(solution)/shard_map/reshape | solution.py:68
  67.8 4.2 copy.51
  72.0 14.8 %all-to-all-start = ((bf16[1,64,4,12,384]{4,2,3,0,1:T(4,128)(2,1)}), bf16[1,64,4,12,384]{4,2,3,0,1:T(4,128)(2,1)}, u32[]{:S(2)}, u32[]{:S(2)}) async-start(bf16[1,64,4,12,384]{4,2,3,0,1:T(4,128)(2,1)} %copy.51), calls=%async_computation | async-start | bytes 4718592 | tf_op jit(solution)/shard_map/all_to_all | solution.py:70
  86.8 5.0 %reshape.197 = bf16[1,256,12,384]{3,2,1,0:T(8,128)(2,1)} reshape(bf16[3072,384]{1,0:T(8,128)(2,1)} %gather_fusion) | data formatting | bytes 4718592 | tf_op jit(solution)/shard_map/vmap()/gather | solution.py:60
  91.8 1.8 fusion.2
  93.8 3.7 fusion.4
  98.1 1.8 broadcast_compare_fusion
  100.2 93.1 %all-to-all-done = bf16[1,64,4,12,384]{4,2,3,0,1:T(4,128)(2,1)} async-done(((bf16[1,64,4,12,384]{4,2,3,0,1:T(4,128)(2,1)}), bf16[1,64,4,12,384]{4,2,3,0,1:T(4,128)(2,1)}, u32[]{:S(2)}, u32[]{:S(2)}) %all-to-all-start) | async-done | bytes 2359328 | tf_op jit(solution)/shard_map/all_to_all | solution.py:70
  193.3 3.3 fusion.16
  196.6 10.4 %fusion.17 = (f32[4,64,12]{1,2,0:T(8,128)S(1)}, f32[4,64,12,64,12]{1,3,4,2,0:T(8,128)}) fusion(bf16[1,64,4,12,128]{4,2,3,0,1:T(4,128)(2,1)S(1)} %get-tuple-element.4, bf16[1,64,4,12,128]{4,2,3,0,1:T(4,128)(2,1)S(1)} %get-tuple-element.3, pred[64,12,64,12]{0,2,3,1:T(8,128)(4,1)S(1)} %copy-done.1, s32[4,64,12]{1,2,0:T(8,128)S(1)} %copy.56, ...), kind=kOutput, calls=%fused_computation.48 | convolution fusion | flops 618132480 | bytes 11627520 | tf_op jit(solution)/shard_map/hscie,htcje->hcsitj/dot_general | solution.py:28
  207.0 10.2 %fusion = f32[4,64,12]{1,2,0:T(8,128)S(1)} fusion(f32[4,64,12,64,12]{1,3,4,2,0:T(8,128)} %get-tuple-element.9, f32[4,64,12]{1,2,0:T(8,128)S(1)} %get-tuple-element.8), kind=kLoop, calls=%fused_computation.5 | loop fusion | flops 4715520 | bytes 9461760 | tf_op jit(solution)/shard_map/reduce_sum | solution.py:38
  217.2 8.5 %fusion.6 = bf16[1,64,4,12,128]{4,1,3,2,0:T(8,128)(2,1)S(1)} fusion(f32[4,64,12,64,12]{1,3,4,2,0:T(8,128)} %get-tuple-element.9, f32[4,64,12]{1,2,0:T(8,128)S(1)} %fusion, f32[4,64,12]{1,2,0:T(8,128)S(1)} %get-tuple-element.8, bf16[1,64,4,12,128]{4,2,3,0,1:T(4,128)(2,1)S(1)} %copy-done.2), kind=kOutput, calls=%fused_computation.16 | convolution fusion | flops 611450880 | bytes 11034624 | tf_op jit(solution)/shard_map/hcsitj,htcje->hscie/dot_general | solution.py:39
  225.8 1.5 copy.61
  227.3 11.4 %all-to-all-start.2 = ((bf16[1,64,4,12,128]{4,2,3,0,1:T(4,128)(2,1)}), bf16[1,64,4,12,128]{4,2,3,0,1:T(4,128)(2,1)}, u32[]{:S(2)}, u32[]{:S(2)}) async-start(bf16[1,64,4,12,128]{4,2,3,0,1:T(4,128)(2,1)} %copy.61), calls=%async_computation.2 | async-start | bytes 1572864 | tf_op jit(solution)/shard_map/all_to_all | solution.py:73
  239.2 136.0 %all-reduce.3.cloned.1.call-done = f32[1,256,128]{2,1,0:T(8,128)} async-done(((f32[1,256,128]{2,1,0:T(8,128)}), f32[1,256,128]{2,1,0:T(8,128)}) %all-reduce.3.cloned.1.call-update) | async-done | bytes 131088 | tf_op jit(solution)/shard_map/psum | solution.py:65
  375.2 0.8 multiply_reduce_fusion.1
  376.0 1.4 copy.62
  377.4 1.1 reshape.208
  378.4 8.6 %scatter_custom_fusion = bf16[1024,128]{1,0:T(8,128)(2,1)S(1)} fusion(s32[3072]{0:T(1024)S(1)} %reshape.206, bf16[3072,128]{1,0:T(8,128)(2,1)} %reshape.208, bf16[]{:T(256)} %constant.15.clone.1), kind=kCustom, calls=%fused_computation.23 | custom fusion | bytes 262656
  387.1 0.5 broadcast.148
  387.6 0.8 reduce.13
  388.4 0.8 reshape.225
  389.2 15.4 %all-to-all-start.3 = ((bf16[8,2,8192]{2,1,0:T(2,128)(2,1)}), bf16[8,2,8192]{2,1,0:T(2,128)(2,1)S(1)}, u32[]{:S(2)}, u32[]{:S(2)}) async-start(bf16[8,2,8192]{2,1,0:T(2,128)(2,1)} %reshape.225), calls=%async_computation.3 | async-start | bytes 524288 | tf_op jit(solution)/shard_map/all_to_all | solution.py:84
  404.6 1.3 dynamic-slice_multiply_fusion
  405.9 5.2 %all-to-all-done.3 = bf16[8,2,8192]{2,1,0:T(2,128)(2,1)S(1)} async-done(((bf16[8,2,8192]{2,1,0:T(2,128)(2,1)}), bf16[8,2,8192]{2,1,0:T(2,128)(2,1)S(1)}, u32[]{:S(2)}, u32[]{:S(2)}) %all-to-all-start.3) | async-done | bytes 262176 | tf_op jit(solution)/shard_map/all_to_all | solution.py:84
  411.4 2.7 fusion.7
  (37 shorter events, 2.2 us)
Async XLA Ops:
  8.0 20.8 %copy-start = (bf16[1024,1024]{1,0:T(8,128)(2,1)S(1)}, bf16[1024,1024]{1,0:T(8,128)(2,1)}, u32[]{:S(2)}) copy-start(bf16[1024,1024]{1,0:T(8,128)(2,1)} %param.5) | copy-start | bytes 6291460
  9.7 62.3 %all-to-all-start.1 = ((s32[1,64,4,12]{3,2,0,1:T(4,128)}), s32[1,64,4,12]{3,2,0,1:T(4,128)S(1)}, u32[]{:S(2)}, u32[]{:S(2)}) async-start(s32[1,64,4,12]{3,2,0,1:T(4,128)} %bitcast.10), calls=%async_computation.1 | async-start | bytes 262144 | tf_op jit(solution)/shard_map/all_to_all | solution.py:71
  72.0 121.4 %all-to-all-start = ((bf16[1,64,4,12,384]{4,2,3,0,1:T(4,128)(2,1)}), bf16[1,64,4,12,384]{4,2,3,0,1:T(4,128)(2,1)}, u32[]{:S(2)}, u32[]{:S(2)}) async-start(bf16[1,64,4,12,384]{4,2,3,0,1:T(4,128)(2,1)} %copy.51), calls=%async_computation | async-start | bytes 4718592 | tf_op jit(solution)/shard_map/all_to_all | solution.py:70
  86.7 6.9 %copy-start.3 = (s32[1,1,256]{2,1,0:T(1,128)S(1)}, s32[1,1,256]{2,1,0:T(1,128)}, u32[]{:S(2)}) copy-start(s32[1,1,256]{2,1,0:T(1,128)} %param.9) | copy-start | bytes 3076
  86.7 288.4 %all-reduce.3.cloned.1.call-start = ((), (), s32[]{:S(2)}) async-start(), calls=%async_computation.5 | async-start | bytes 262144 | tf_op jit(solution)/shard_map/psum | solution.py:65
  97.5 313.9 %all-gather.2.cloned.1.call-start = ((), (), s32[]{:S(2)}) async-start(), calls=%async_computation.4 | async-start | bytes 2359296 | tf_op jit(solution)/shard_map/all_gather | solution.py:88
  100.2 96.4 %copy-start.1 = (pred[64,12,64,12]{0,2,3,1:T(8,128)(4,1)S(1)}, pred[64,12,64,12]{0,2,3,1:T(8,128)(4,1)}, u32[]{:S(2)}) copy-start(pred[64,12,64,12]{0,2,3,1:T(8,128)(4,1)} %broadcast_compare_fusion) | copy-start | bytes 1769476
  207.0 10.2 %copy-start.2 = (bf16[1,64,4,12,128]{4,2,3,0,1:T(4,128)(2,1)S(1)}, bf16[1,64,4,12,128]{4,2,3,0,1:T(4,128)(2,1)}, u32[]{:S(2)}) copy-start(bf16[1,64,4,12,128]{4,2,3,0,1:T(4,128)(2,1)} %get-tuple-element.2) | copy-start | bytes 2359300
  225.7 12.9 %copy-start.4 = (s32[2]{0:T(128)S(1)}, s32[2]{0:T(128)}, u32[]{:S(2)}) copy-start(s32[2]{0:T(128)} %constant.45) | copy-start | bytes 28
  225.7 13.0 %copy-start.5 = (s32[2]{0:T(128)S(1)}, s32[2]{0:T(128)}, u32[]{:S(2)}) copy-start(s32[2]{0:T(128)} %constant.48) | copy-start | bytes 28
  227.3 148.7 %all-to-all-start.2 = ((bf16[1,64,4,12,128]{4,2,3,0,1:T(4,128)(2,1)}), bf16[1,64,4,12,128]{4,2,3,0,1:T(4,128)(2,1)}, u32[]{:S(2)}, u32[]{:S(2)}) async-start(bf16[1,64,4,12,128]{4,2,3,0,1:T(4,128)(2,1)} %copy.61), calls=%async_computation.2 | async-start | bytes 1572864 | tf_op jit(solution)/shard_map/all_to_all | solution.py:73
  389.2 21.9 %all-to-all-start.3 = ((bf16[8,2,8192]{2,1,0:T(2,128)(2,1)}), bf16[8,2,8192]{2,1,0:T(2,128)(2,1)S(1)}, u32[]{:S(2)}, u32[]{:S(2)}) async-start(bf16[8,2,8192]{2,1,0:T(2,128)(2,1)} %reshape.225), calls=%async_computation.3 | async-start | bytes 524288 | tf_op jit(solution)/shard_map/all_to_all | solution.py:84
Sparse Core Ops, SparseCore 0:
  97.6 277.4 all-reduce.2
Sparse Core Ops, SparseCore 1:
  100.1 35.2 all-gather.1
where the time goes:
time: 423 us; the launch traced here: 422 us
  waiting for transfers between devices  235 us (56%)
  local copies, waits for them, and re-layouts  63.8 us (15%)
  starting transfers between devices  60.9 us (14%)
  matrix products  24.6 us (6%)
  other arithmetic  21.9 us (5%)
  between operations  15.7 us (4%)
    psum x1, waiting for transfers between devices, on_device(): all_sums = lax.psum(slab_sums, 'seq')  136 us
    all_to_all x1, waiting for transfers between devices, on_device(): lax.all_to_all(send_rows, 'seq', split_axis=1, concat_axis=1, tiled=True)  93.1 us
    gather x4, local copies, waits for them, and re-layouts, on_device(): table[index]  34.3 us
    all_to_all x1, starting transfers between devices, on_device(): lax.all_to_all(send_positions, 'seq', split_axis=1, concat_axis=1, tiled=...  19.1 us
    all_to_all x1, starting transfers between devices, on_device(): lax.all_to_all(head_out, 'head', split_axis=0, concat_axis=1, tiled=True)  15.4 us
    all_to_all x1, starting transfers between devices, on_device(): lax.all_to_all(send_rows, 'seq', split_axis=1, concat_axis=1, tiled=True)  14.8 us
    all_to_all x1, starting transfers between devices, on_device(): lax.all_to_all(attended, 'seq', split_axis=1, concat_axis=1, tiled=True)  11.4 us
    dot_general x1, matrix products, attend_core(): jnp.einsum('hscie,htcje->hcsitj', queries, keys_in, preferred_element_typ...  10.4 us
  transfers between devices with their start and end apart: 6, of which 3 were waited for; matrix products, arithmetic and copies ran while one was open for 25% of the time, Pallas kernels for 0%

commit v1 on v0

--- a/solution.py
+++ b/solution.py
@@ -62,7 +62,7 @@
         jnp.where(valid[..., None], unit_rows(member_rows[..., head_dim : 2 * head_dim]), 0.0),
         axis=2,
     )
-    all_sums = lax.psum(slab_sums, "seq")
+    all_sums = jnp.sum(lax.all_gather(slab_sums, "seq"), axis=0)
     mine = lax.dynamic_slice_in_dim(all_sums, my_slab * owned, owned, 1)
     head_index = jnp.arange(heads_here, dtype=jnp.int32)[:, None, None]
     send_rows = member_rows.reshape(heads_here, seq_count, owned, slab_slots, 3 * head_dim)

time: 423 us -> 342 us (0.81)
  waiting for transfers between devices: 235 us -> 162 us
  starting transfers between devices: 60.9 us -> 51.7 us
    psum x1 -> x0, waiting for transfers between devices: 136 us -> none  [on_device(): all_sums = lax.psum(slab_sums, 'seq')]
    all_to_all x1, waiting for transfers between devices: 0.01 us -> 51.4 us  [on_device(): lax.all_to_all(attended, 'seq', split_axis=1, concat_axis=1, tiled=True)]
    all_to_all x1, waiting for transfers between devices: 93.1 us -> 103 us  [on_device(): lax.all_to_all(send_rows, 'seq', split_axis=1, concat_axis=1, tiled=True)]
    all_to_all x1, starting transfers between devices: 15.4 us -> 5.99 us  [on_device(): lax.all_to_all(head_out, 'head', split_axis=0, concat_axis=1, tiled=True)]
  transfers between devices with their start and end apart: 6 -> 6, of which waited for: 3 -> 3; matrix products, arithmetic and copies ran while one was open for 25% -> 32% of each run, Pallas kernels for 0% -> 0%
where the time goes in v1:
time: 342 us; the launch traced here: 341 us
  waiting for transfers between devices  162 us (47%)
  local copies, waits for them, and re-layouts  63.8 us (19%)
  starting transfers between devices  51.7 us (15%)
  matrix products  24.9 us (7%)
  other arithmetic  24.3 us (7%)
  between operations  14.3 us (4%)
    all_to_all x1, waiting for transfers between devices, on_device(): lax.all_to_all(send_rows, 'seq', split_axis=1, concat_axis=1, tiled=True)  103 us
    all_to_all x1, waiting for transfers between devices, on_device(): lax.all_to_all(attended, 'seq', split_axis=1, concat_axis=1, tiled=True)  51.4 us
    gather x4, local copies, waits for them, and re-layouts, on_device(): table[index]  34.3 us
    all_to_all x1, starting transfers between devices, on_device(): lax.all_to_all(send_positions, 'seq', split_axis=1, concat_axis=1, tiled=...  19.1 us
    all_to_all x1, starting transfers between devices, on_device(): lax.all_to_all(send_rows, 'seq', split_axis=1, concat_axis=1, tiled=True)  14.7 us
    all_to_all x1, starting transfers between devices, on_device(): lax.all_to_all(attended, 'seq', split_axis=1, concat_axis=1, tiled=True)  11.6 us
    dot_general x1, matrix products, attend_core(): jnp.einsum('hscie,htcje->hcsitj', queries, keys_in, preferred_element_typ...  10.4 us
    reduce_sum x1, other arithmetic, attend_core(): jnp.sum(expo, axis=(4, 5), keepdims=True)  10.3 us
  transfers between devices with their start and end apart: 6, of which 3 were waited for; matrix products, arithmetic and copies ran while one was open for 32% of the time, Pallas kernels for 0%

profile of v1, /device:TPU:1, one launch (start us, length us, event | category | flops | bytes accessed | tf_op | source)
XLA Modules:
  0.0 340.5 jit_solution(10861600883006723776)
XLA Ops:
  7.2 0.7 all-gather.4.cloned.1.call-update
  7.9 0.7 compare_select_fusion.2
  8.7 0.8 copy.69
  9.4 19.1 %all-to-all-start.1 = ((s32[1,64,4,12]{3,2,0,1:T(4,128)}), s32[1,64,4,12]{3,2,0,1:T(4,128)S(1)}, u32[]{:S(2)}, u32[]{:S(2)}) async-start(s32[1,64,4,12]{3,2,0,1:T(4,128)} %bitcast.10), calls=%async_computation.1 | async-start | bytes 262144 | tf_op jit(solution)/shard_map/all_to_all | solution.py:71
  28.6 3.0 fusion.5
  31.9 1.5 copy.66
  33.5 29.1 %gather_fusion = bf16[3072,384]{1,0:T(8,128)(2,1)} fusion(bf16[1,1024,384]{2,1,0:T(8,128)(2,1)S(1)} %copy.66, s32[3072]{0:T(1024)S(1)} %reshape.204), kind=kCustom, calls=%fused_computation | custom fusion | bytes 4743168 | tf_op jit(solution)/shard_map/vmap()/gather | solution.py:60
  62.6 5.0 %reshape.186 = bf16[1,64,4,12,384]{4,3,2,1,0:T(8,128)(2,1)} reshape(bf16[3072,384]{1,0:T(8,128)(2,1)} %gather_fusion) | data formatting | bytes 4718592 | tf_op jit(solution)/shard_map/reshape | solution.py:68
  67.5 4.2 %copy.67 = bf16[1,64,4,12,384]{4,2,3,0,1:T(4,128)(2,1)} copy(bf16[1,64,4,12,384]{4,3,2,1,0:T(8,128)(2,1)} %reshape.186) | data formatting | bytes 4718592 | tf_op jit(solution)/shard_map/reshape | solution.py:68
  71.8 14.7 %all-to-all-start = ((bf16[1,64,4,12,384]{4,2,3,0,1:T(4,128)(2,1)}), bf16[1,64,4,12,384]{4,2,3,0,1:T(4,128)(2,1)}, u32[]{:S(2)}, u32[]{:S(2)}) async-start(bf16[1,64,4,12,384]{4,2,3,0,1:T(4,128)(2,1)} %copy.67), calls=%async_computation | async-start | bytes 4718592 | tf_op jit(solution)/shard_map/all_to_all | solution.py:70
  86.7 5.0 %reshape.203 = bf16[1,256,12,384]{3,2,1,0:T(8,128)(2,1)} reshape(bf16[3072,384]{1,0:T(8,128)(2,1)} %gather_fusion) | data formatting | bytes 4718592 | tf_op jit(solution)/shard_map/vmap()/gather | solution.py:60
  91.7 1.8 fusion.2
  93.7 3.7 %fusion.4 = f32[256,128]{1,0:T(8,128)} fusion(f32[256,12]{1,0:T(8,128)S(1)} %add_rsqrt_fusion, pred[256,12]{1,0:T(8,128)(4,1)S(1)} %iota_compare_fusion, bf16[1,256,12,384]{3,2,1,0:T(8,128)(2,1)} %reshape.203), kind=kLoop, calls=%fused_computation.12 | loop fusion | flops 1540096 | bytes 932864 | tf_op jit(solution)/shard_map/reduce_sum | solution.py:61
  97.5 1.8 broadcast_compare_fusion
  99.6 102.9 %all-to-all-done = bf16[1,64,4,12,384]{4,2,3,0,1:T(4,128)(2,1)} async-done(((bf16[1,64,4,12,384]{4,2,3,0,1:T(4,128)(2,1)}), bf16[1,64,4,12,384]{4,2,3,0,1:T(4,128)(2,1)}, u32[]{:S(2)}, u32[]{:S(2)}) %all-to-all-start) | async-done | bytes 2359328 | tf_op jit(solution)/shard_map/all_to_all | solution.py:70
  202.5 3.3 fusion.16
  205.8 10.4 %fusion.17 = (f32[4,64,12]{1,2,0:T(8,128)S(1)}, f32[4,64,12,64,12]{1,3,4,2,0:T(8,128)}) fusion(bf16[1,64,4,12,128]{4,2,3,0,1:T(4,128)(2,1)S(1)} %get-tuple-element.4, bf16[1,64,4,12,128]{4,2,3,0,1:T(4,128)(2,1)S(1)} %get-tuple-element.3, pred[64,12,64,12]{0,2,3,1:T(8,128)(4,1)S(1)} %copy-done.1, s32[4,64,12]{1,2,0:T(8,128)S(1)} %copy.72, ...), kind=kOutput, calls=%fused_computation.48 | convolution fusion | flops 618132480 | bytes 11627520 | tf_op jit(solution)/shard_map/hscie,htcje->hcsitj/dot_general | solution.py:28
  216.2 10.3 %fusion = f32[4,64,12]{1,2,0:T(8,128)S(1)} fusion(f32[4,64,12,64,12]{1,3,4,2,0:T(8,128)} %get-tuple-element.9, f32[4,64,12]{1,2,0:T(8,128)S(1)} %get-tuple-element.8), kind=kLoop, calls=%fused_computation.5 | loop fusion | flops 4715520 | bytes 9461760 | tf_op jit(solution)/shard_map/reduce_sum | solution.py:38
  226.5 8.7 %fusion.6 = bf16[1,64,4,12,128]{4,1,3,2,0:T(8,128)(2,1)S(1)} fusion(f32[4,64,12,64,12]{1,3,4,2,0:T(8,128)} %get-tuple-element.9, f32[4,64,12]{1,2,0:T(8,128)S(1)} %fusion, f32[4,64,12]{1,2,0:T(8,128)S(1)} %get-tuple-element.8, bf16[1,64,4,12,128]{4,2,3,0,1:T(4,128)(2,1)S(1)} %copy-done.2), kind=kOutput, calls=%fused_computation.16 | convolution fusion | flops 611450880 | bytes 11034624 | tf_op jit(solution)/shard_map/hcsitj,htcje->hscie/dot_general | solution.py:39
  235.3 1.5 copy.77
  236.8 11.6 %all-to-all-start.2 = ((bf16[1,64,4,12,128]{4,2,3,0,1:T(4,128)(2,1)}), bf16[1,64,4,12,128]{4,2,3,0,1:T(4,128)(2,1)}, u32[]{:S(2)}, u32[]{:S(2)}) async-start(bf16[1,64,4,12,128]{4,2,3,0,1:T(4,128)(2,1)} %copy.77), calls=%async_computation.2 | async-start | bytes 1572864 | tf_op jit(solution)/shard_map/all_to_all | solution.py:73
  248.9 51.4 %all-to-all-done.2 = bf16[1,64,4,12,128]{4,2,3,0,1:T(4,128)(2,1)} async-done(((bf16[1,64,4,12,128]{4,2,3,0,1:T(4,128)(2,1)}), bf16[1,64,4,12,128]{4,2,3,0,1:T(4,128)(2,1)}, u32[]{:S(2)}, u32[]{:S(2)}) %all-to-all-start.2) | async-done | bytes 786464 | tf_op jit(solution)/shard_map/all_to_all | solution.py:73
  300.3 1.4 copy.78
  301.8 1.1 reshape.214
  302.8 8.6 %scatter_custom_fusion = bf16[1024,128]{1,0:T(8,128)(2,1)S(1)} fusion(s32[3072]{0:T(1024)S(1)} %reshape.212, bf16[3072,128]{1,0:T(8,128)(2,1)} %reshape.214, bf16[]{:T(256)} %constant.15.clone.1), kind=kCustom, calls=%fused_computation.23 | custom fusion | bytes 262656
  312.0 0.8 reduce.17
  312.8 0.8 reshape.233
  313.5 6.0 %all-to-all-start.3 = ((bf16[8,2,8192]{2,1,0:T(2,128)(2,1)}), bf16[8,2,8192]{2,1,0:T(2,128)(2,1)S(1)}, u32[]{:S(2)}, u32[]{:S(2)}) async-start(bf16[8,2,8192]{2,1,0:T(2,128)(2,1)} %reshape.233), calls=%async_computation.3 | async-start | bytes 524288 | tf_op jit(solution)/shard_map/all_to_all | solution.py:84
  319.5 6.5 %all-to-all-done.3 = bf16[8,2,8192]{2,1,0:T(2,128)(2,1)S(1)} async-done(((bf16[8,2,8192]{2,1,0:T(2,128)(2,1)}), bf16[8,2,8192]{2,1,0:T(2,128)(2,1)S(1)}, u32[]{:S(2)}, u32[]{:S(2)}) %all-to-all-start.3) | async-done | bytes 262176 | tf_op jit(solution)/shard_map/all_to_all | solution.py:84
  326.4 2.7 fusion.7
  329.1 3.8 %reduce.14 = f32[256,128]{1,0:T(8,128)S(1)} reduce(f32[64,256,128]{2,1,0:T(8,128)} %bitcast.73, f32[]{:T(128)} %constant.11.clone.1), dimensions={0}, to_apply=%region_5.6 | reduce | flops 2064384 | bytes 8519684 | tf_op jit(solution)/shard_map/reduce_sum | solution.py:65
  333.0 0.7 multiply_bitcast_fusion
  (38 shorter events, 2.5 us)
Async XLA Ops:
  7.2 21.4 %copy-start = (bf16[1024,1024]{1,0:T(8,128)(2,1)S(1)}, bf16[1024,1024]{1,0:T(8,128)(2,1)}, u32[]{:S(2)}) copy-start(bf16[1024,1024]{1,0:T(8,128)(2,1)} %param.5) | copy-start | bytes 6291460
  7.2 319.2 %all-gather.4.cloned.1.call-start = ((), (), s32[]{:S(2)}) async-start(), calls=%async_computation.4 | async-start | bytes 2359296 | tf_op jit(solution)/shard_map/all_gather | solution.py:88
  9.4 62.3 %all-to-all-start.1 = ((s32[1,64,4,12]{3,2,0,1:T(4,128)}), s32[1,64,4,12]{3,2,0,1:T(4,128)S(1)}, u32[]{:S(2)}, u32[]{:S(2)}) async-start(s32[1,64,4,12]{3,2,0,1:T(4,128)} %bitcast.10), calls=%async_computation.1 | async-start | bytes 262144 | tf_op jit(solution)/shard_map/all_to_all | solution.py:71
  71.8 130.7 %all-to-all-start = ((bf16[1,64,4,12,384]{4,2,3,0,1:T(4,128)(2,1)}), bf16[1,64,4,12,384]{4,2,3,0,1:T(4,128)(2,1)}, u32[]{:S(2)}, u32[]{:S(2)}) async-start(bf16[1,64,4,12,384]{4,2,3,0,1:T(4,128)(2,1)} %copy.67), calls=%async_computation | async-start | bytes 4718592 | tf_op jit(solution)/shard_map/all_to_all | solution.py:70
  86.5 7.1 %copy-start.3 = (s32[1,1,256]{2,1,0:T(1,128)S(1)}, s32[1,1,256]{2,1,0:T(1,128)}, u32[]{:S(2)}) copy-start(s32[1,1,256]{2,1,0:T(1,128)} %param.9) | copy-start | bytes 3076
  86.5 242.6 %all-gather.6.cloned.1.call-start = ((), (), s32[]{:S(2)}) async-start(), calls=%async_computation.5 | async-start | bytes 8519680 | tf_op jit(solution)/shard_map/all_gather | solution.py:65
  99.5 106.4 %copy-start.1 = (pred[64,12,64,12]{0,2,3,1:T(8,128)(4,1)S(1)}, pred[64,12,64,12]{0,2,3,1:T(8,128)(4,1)}, u32[]{:S(2)}) copy-start(pred[64,12,64,12]{0,2,3,1:T(8,128)(4,1)} %broadcast_compare_fusion) | copy-start | bytes 1769476
  216.2 10.3 %copy-start.2 = (bf16[1,64,4,12,128]{4,2,3,0,1:T(4,128)(2,1)S(1)}, bf16[1,64,4,12,128]{4,2,3,0,1:T(4,128)(2,1)}, u32[]{:S(2)}) copy-start(bf16[1,64,4,12,128]{4,2,3,0,1:T(4,128)(2,1)} %get-tuple-element.2) | copy-start | bytes 2359300
  235.2 13.2 %copy-start.4 = (s32[2]{0:T(128)S(1)}, s32[2]{0:T(128)}, u32[]{:S(2)}) copy-start(s32[2]{0:T(128)} %constant.45) | copy-start | bytes 28
  235.3 13.3 %copy-start.5 = (s32[2]{0:T(128)S(1)}, s32[2]{0:T(128)}, u32[]{:S(2)}) copy-start(s32[2]{0:T(128)} %constant.48) | copy-start | bytes 28
  236.8 63.6 %all-to-all-start.2 = ((bf16[1,64,4,12,128]{4,2,3,0,1:T(4,128)(2,1)}), bf16[1,64,4,12,128]{4,2,3,0,1:T(4,128)(2,1)}, u32[]{:S(2)}, u32[]{:S(2)}) async-start(bf16[1,64,4,12,128]{4,2,3,0,1:T(4,128)(2,1)} %copy.77), calls=%async_computation.2 | async-start | bytes 1572864 | tf_op jit(solution)/shard_map/all_to_all | solution.py:73
  313.5 12.5 %all-to-all-start.3 = ((bf16[8,2,8192]{2,1,0:T(2,128)(2,1)}), bf16[8,2,8192]{2,1,0:T(2,128)(2,1)S(1)}, u32[]{:S(2)}, u32[]{:S(2)}) async-start(bf16[8,2,8192]{2,1,0:T(2,128)(2,1)} %reshape.233), calls=%async_computation.3 | async-start | bytes 524288 | tf_op jit(solution)/shard_map/all_to_all | solution.py:84
Sparse Core Ops, SparseCore 0:
  10.2 38.5 all-gather.3
  97.6 213.5 all-gather.5
